TPU v7x, 32 devices: a whole 2x2x4 slice. The times are simulated.
32 devices in a mesh: span: 8 (over z, y), cross: 4 (over x, core).
Axes of the slice: x: 2, y: 2, z: 4, core: 2. Of those that a mesh axis runs over, the one named last changes fastest.
Arguments:
- divergence: float32 [64, 128, 256], P('span', 'cross'), may hold values from -6 to 6
- inverse_density: float32 [64, 128, 256], P('span', 'cross'), may hold values from 0.5 to 2
Outputs:
- pressure: float32 [64, 128, 256], P('span', 'cross')
- residual: float32 [64, 128, 256], P('span', 'cross')
All inputs are finite; a program needn't handle non-finite values.
Results may differ from a plain program's by a relative error of at most 0.0002.
Values sent between devices are 32-bit elements; how exact they have to be, the bound alone decides.
A program may use at most 64 MiB of HBM per device.

v0:
```python
import functools

import jax
import jax.numpy as jnp
from jax import lax
from jax.experimental import pallas as pl
from jax.experimental.pallas import tpu as pltpu
from jax.sharding import PartitionSpec as P

ITERS_C = 64
RELAX = 0.8
KEEP = 1.0 - RELAX
HF = 3
HM = 4
PAD = 8
DIRS = [(dx, dy) for dx in (-1, 0, 1) for dy in (-1, 0, 1) if (dx, dy) != (0, 0)]
HI = lax.Precision.HIGHEST
F32 = jnp.float32


def dot(a, b):
    return jnp.dot(a, b, precision=HI, preferred_element_type=F32)


def select_matrix(rows, cols, test):
    r = lax.broadcasted_iota(jnp.int32, (rows, cols), 0)
    c = lax.broadcasted_iota(jnp.int32, (rows, cols), 1)
    return jnp.where(test(r, c), 1.0, 0.0).astype(F32)


def kernel(S, C, b_hbm, k_hbm, p_out, r_out,
           K, B, U, V, W, DD, UE, K1, B1, U1, V1, W1, D1, UE1,
           stage, GK, GB, KP, va, vb, wts, t256, t128,
           corner_out, corner_in, FF, F1,
           load_sem, send_f, recv_f, send_m, recv_m, send_g, recv_g, send_c, recv_c, known):
    depth, rows, cols = b_hbm.shape
    FY = rows + 2 * PAD
    mdepth, mrows, mcols = depth // 2, rows // 2, cols // 2
    MY = mrows + 2 * PAD
    crows = mrows // 2
    CR = crows * C
    half = mcols // 2
    s = lax.axis_index("span")
    c = lax.axis_index("cross")

    loads = [
        pltpu.make_async_copy(k_hbm, K.at[pl.ds(HF, depth), pl.ds(PAD, rows), :], load_sem.at[0]),
        pltpu.make_async_copy(b_hbm, B.at[pl.ds(HF, depth), pl.ds(PAD, rows), :], load_sem.at[1]),
    ]
    for x in loads:
        x.start()

    peers = [(i, j) for i in range(S) for j in range(C) if (i, j) != (0, 0)]

    def peer(o):
        return (lax.rem(s + o[0], S), lax.rem(c + o[1], C))


    def exists(dx, dy):
        return (s + dx >= 0) & (s + dx < S) & (c + dy >= 0) & (c + dy < C)

    def greet(sem, step):
        for dx, dy in DIRS:
            @pl.when(exists(dx * step, dy * step))
            def _(dx=dx, dy=dy):
                pl.semaphore_signal(
                    sem, inc=1, device_id=(s + dx * step, c + dy * step), device_id_type=pl.DeviceIdType.MESH
                )

    def heard(sem, step):
        present = [jnp.where(exists(dx * step, dy * step), 1, 0) for dx, dy in DIRS]
        pl.semaphore_wait(sem, sum(present))

    barrier = pltpu.get_barrier_semaphore()
    greet(barrier, 1)

    def spans(dx, dy, halo, h0, h1, n, r):
        if dx == 0:
            sl, dl, ln = halo, halo, n
        elif dx == 1:
            sl, dl, ln = halo + n - h1, halo - h1, h1 - h0
        else:
            sl, dl, ln = halo + h0, halo + n + h0, h1 - h0
        if dy == 0:
            sr, dr, rn = PAD, PAD, r
        elif dy == 1:
            sr, dr, rn = PAD + r - PAD, 0, PAD
        else:
            sr, dr, rn = PAD, PAD + r, PAD
        return sl, dl, ln, sr, dr, rn

    class Exchange:
        def __init__(self, buf, halo, h0, h1, n, r, ssem, rsem, slot, source=None, corners=True):
            self.items = []
            for q, (dx, dy) in enumerate(DIRS):
                if (dx == 0 and h0 > 0) or (dx != 0 and dy != 0 and not corners):
                    continue
                sl, dl, ln, sr, dr, rn = spans(dx, dy, halo, h0, h1, n, r)
                if source is None:
                    src = buf.at[pl.ds(sl, ln), pl.ds(sr, rn), :]
                else:
                    src = source.at[pl.ds(sl - halo, ln), pl.ds(sr - PAD, rn), :]
                copy = pltpu.make_async_remote_copy(
                    src_ref=src,
                    dst_ref=buf.at[pl.ds(dl, ln), pl.ds(dr, rn), :],
                    send_sem=ssem.at[slot, q],
                    recv_sem=rsem.at[slot, q],
                    device_id=(jnp.clip(s + dx, 0, S - 1), jnp.clip(c + dy, 0, C - 1)),
                    device_id_type=pl.DeviceIdType.MESH,
                )
                self.items.append((dx, dy, copy))

        def start(self):
            for dx, dy, copy in self.items:
                @pl.when(exists(dx, dy))
                def _(copy=copy):
                    copy.start()

        def wait_recv(self, span=None):
            for dx, dy, copy in self.items:
                if span is not None and span != abs(dx):
                    continue

                @pl.when(exists(-dx, -dy))
                def _(copy=copy):
                    copy.wait_recv()

        def wait_send(self):
            for dx, dy, copy in self.items:
                @pl.when(exists(dx, dy))
                def _(copy=copy):
                    copy.wait_send()

    def zero_edges(buf, halo, n, r):
        total = buf.shape[1]
        width = buf.shape[2]

        @pl.when(s == 0)
        def _():
            buf[0:halo] = jnp.zeros((halo, total, width), F32)

        @pl.when(s == S - 1)
        def _():
            buf[halo + n:] = jnp.zeros((halo, total, width), F32)

        @pl.when(c == 0)
        def _():
            buf[:, 0:PAD, :] = jnp.zeros((n + 2 * halo, PAD, width), F32)

        @pl.when(c == C - 1)
        def _():
            buf[:, PAD + r:, :] = jnp.zeros((n + 2 * halo, PAD, width), F32)

    class Corners:
        def __init__(self, slot, bufs):
            self.slot, self.bufs, self.items = slot, bufs, []
            for q, (dx, dy) in enumerate((i, j) for i in (-1, 1) for j in (-1, 1)):
                copy = pltpu.make_async_remote_copy(
                    src_ref=corner_out.at[slot, q],
                    dst_ref=corner_in.at[slot, q],
                    send_sem=send_c.at[slot, q],
                    recv_sem=recv_c.at[slot, q],
                    device_id=(jnp.clip(s + dx, 0, S - 1), jnp.clip(c + dy, 0, C - 1)),
                    device_id_type=pl.DeviceIdType.MESH,
                )
                self.items.append((q, dx, dy, copy))

        def pack(self):
            for q, dx, dy, copy in self.items:
                at = 0
                for buf in self.bufs:
                    for e in range(2):
                        layer = HF + depth - 1 - e if dx == 1 else HF + e
                        row = PAD + rows - 2 if dy == 1 else PAD
                        corner_out[self.slot, q, at:at + 2, :] = buf[layer, row:row + 2, :]
                        at += 2

        def start(self):
            for q, dx, dy, copy in self.items:
                @pl.when(exists(dx, dy))
                def _(copy=copy):
                    copy.start()

        def receive(self):
            for q, dx, dy, copy in self.items:
                @pl.when(exists(-dx, -dy))
                def _(q=q, dx=dx, dy=dy, copy=copy):
                    copy.wait_recv()
                    at = 0
                    for buf in self.bufs:
                        for e in range(2):
                            layer = HF - 1 - e if dx == 1 else HF + depth + e
                            row = PAD - 2 if dy == 1 else PAD + rows
                            buf[layer, row:row + 2, :] = corner_in[self.slot, q, at:at + 2, :]
                            at += 2

        def wait_send(self):
            for q, dx, dy, copy in self.items:
                @pl.when(exists(dx, dy))
                def _(copy=copy):
                    copy.wait_send()

    heard(barrier, 1)
    ek = Exchange(K, HF, 0, 3, depth, rows, send_f, recv_f, 0, k_hbm, corners=False)
    eb = Exchange(B, HF, 0, 2, depth, rows, send_f, recv_f, 1, b_hbm, corners=False)
    ek.start()
    eb.start()
    corner_out[...] = jnp.zeros(corner_out.shape, F32)
    for x in loads:
        x.wait()
    ec = Corners(0, (K, B))
    ec.pack()
    ec.start()

    step, turn = 1, 0
    while step < max(S, C) - 1:
        greet(known.at[turn], step)
        heard(known.at[turn], step)
        step, turn = 2 * step, turn + 1

    for buf in (K, B, UE):
        for i in (0, HF + depth):
            for j in (0, PAD + rows):
                buf[i:i + HF, j:j + PAD, :] = jnp.zeros((HF, PAD, cols), F32)
        zero_edges(buf, HF, depth, rows)
    for buf in (K1, B1, UE1):
        zero_edges(buf, HM, mdepth, mrows)
    KP[...] = jnp.zeros(KP.shape, F32)
    va[...] = jnp.zeros(va.shape, F32)
    vb[...] = jnp.zeros(vb.shape, F32)

    pair_z = select_matrix(cols, mcols, lambda r, q: (r == 2 * q) | (r == 2 * q + 1))
    low = [
        select_matrix(mcols, mcols, lambda r, q, p=p: (r == 2 * (q - p * half)) | (r == 2 * (q - p * half) + 1))
        for p in range(2)
    ]

    def restrict_rows(n):
        return t128[pl.ds(0, n, stride=2), :] + t128[pl.ds(1, n, stride=2), :]

    def to_low(mid):
        n = (mdepth // 2) * mrows
        for j in range(mdepth // 2):
            t128[j * mrows:(j + 1) * mrows, :] = mid(2 * j) + mid(2 * j + 1)
        packed = restrict_rows(n // 2)
        return dot(packed[0:crows], low[0]) + dot(packed[crows:2 * crows], low[1])

    for j in range(mdepth):
        t256[j * rows:(j + 1) * rows, :] = (
            K[HF + 2 * j, pl.ds(PAD, rows), :] + K[HF + 2 * j + 1, pl.ds(PAD, rows), :]
        )
    t128[...] = dot(t256[...], pair_z)
    K1[HM:HM + mdepth, PAD:PAD + mrows, :] = (0.125 * restrict_rows(mdepth * mrows)).reshape(mdepth, mrows, mcols)
    ek1 = Exchange(K1, HM, 0, HM, mdepth, mrows, send_m, recv_m, 0)

    def gather(slot, dst):
        row = pl.multiple_of(c * crows, crows)
        return [
            pltpu.make_async_remote_copy(
                src_ref=stage.at[slot],
                dst_ref=dst.at[s, pl.ds(row, crows), :],
                send_sem=send_g.at[slot, n],
                recv_sem=recv_g.at[slot, n],
                device_id=peer(o),
                device_id_type=pl.DeviceIdType.MESH,
            )
            for n, o in reversed(list(enumerate(peers)))
        ]

    def own_block(dst, value):
        dst[s, pl.ds(pl.multiple_of(c * crows, crows), crows), :] = value

    k2 = 0.125 * to_low(lambda j: K1[HM + j, pl.ds(PAD, mrows), :])
    stage[0] = k2
    gk = gather(0, GK)
    own_block(GK, k2)

    def coupling(Kr, Fr, Vr, i):
        k0, v0 = Kr[i], Vr[i]
        n, m = v0.shape
        x = (k0 + Kr[i - 1]) * Vr[i - 1] + (k0 + Kr[i + 1]) * Vr[i + 1]
        y = Fr[0, i] * pltpu.roll(v0, 1, 0) + Fr[1, i] * pltpu.roll(v0, n - 1, 0)
        z = Fr[2, i] * pltpu.roll(v0, 1, 1) + Fr[3, i] * pltpu.roll(v0, m - 1, 1)
        return x + (y + z)

    def diagonal(Kr, Fr, i, factor, halo, n, r):
        k0 = Kr[i]
        height, m = k0.shape
        lane = lax.broadcasted_iota(jnp.int32, k0.shape, 1)
        y0, y1 = pltpu.roll(k0, 1, 0), pltpu.roll(k0, height - 1, 0)
        z0 = jnp.where(lane == 0, 0.0, pltpu.roll(k0, 1, 1))
        z1 = jnp.where(lane == m - 1, 0.0, pltpu.roll(k0, m - 1, 1))
        Fr[0, i] = k0 + y0
        Fr[1, i] = k0 + y1
        Fr[2, i] = jnp.where(lane == 0, 0.0, k0 + z0)
        Fr[3, i] = jnp.where(lane == m - 1, 0.0, k0 + z1)
        total = factor * (6.0 * k0 + ((Kr[i - 1] + Kr[i + 1]) + ((y0 + y1) + (z0 + z1))))
        y = lax.broadcasted_iota(jnp.int32, k0.shape, 0) + (c * r - PAD)
        inside = (y >= 0) & (y < r * C)
        x = s * n - halo + i
        xin = jnp.where((x >= 0) & (x < n * S), 1.0, 0.0).astype(F32)
        total = jnp.where(inside, total, 1.0) + (1.0 - xin)
        return total, jnp.where(inside, RELAX / total, 0.0) * xin

    def sweep(Kr, Fr, Br, Wr, src, dst, factor, layers):
        for i in layers:
            dst[i] = KEEP * src[i] + Wr[i] * (Br[i] + factor * coupling(Kr, Fr, src, i))

    def split(lo, hi, inner_lo, inner_hi):
        return list(range(inner_lo, inner_hi)), [i for i in range(lo, hi) if not inner_lo <= i < inner_hi]

    def fine_start(layers):
        for i in layers:
            total, inv = diagonal(K, FF, i, 0.5, HF, depth, rows)
            DD[i] = total
            W[i] = inv
            U[i] = B[i] * inv

    own = pl.ds(PAD, rows)

    def fine_residual(i):
        return B[i] - DD[i] * V[i] + 0.5 * coupling(K, FF, V, i)

    def fine_pairs(pairs):
        for j in pairs:
            i = HF + 2 * j
            both = fine_residual(i) + fine_residual(i + 1)
            t256[j * rows:(j + 1) * rows, :] = both[PAD:PAD + rows]

    end = HF + depth
    in_d, out_d = split(HF - 2, end + 2, HF + 1, end - 1)
    in_u, out_u = split(HF - 1, end + 1, HF + 2, end - 2)
    in_r, out_r = split(0, mdepth, 2, mdepth - 2)
    ek.wait_recv(0)
    eb.wait_recv(0)
    fine_start(in_d)
    sweep(K, FF, B, W, U, V, 0.5, in_u)
    fine_pairs(in_r)
    ek.wait_recv(1)
    eb.wait_recv(1)
    ec.receive()
    ek1.start()
    for x in gk:
        x.start()
    fine_start(out_d)
    sweep(K, FF, B, W, U, V, 0.5, out_u)
    fine_pairs(out_r)

    t128[...] = dot(t256[...], pair_z)
    B1[HM:HM + mdepth, PAD:PAD + mrows, :] = restrict_rows(mdepth * mrows).reshape(mdepth, mrows, mcols)
    eb1 = Exchange(B1, HM, 0, 2, mdepth, mrows, send_m, recv_m, 1)
    eb1.start()

    UE[HF:HF + depth, PAD:PAD + rows, :] = V[HF:HF + depth, PAD:PAD + rows, :]
    ek1.wait_recv()

    for i in range(HM - 3, HM + mdepth + 3):
        total, inv = diagonal(K1, F1, i, 1.0, HM, mdepth, mrows)
        D1[i] = total
        W1[i] = inv

    for x in gk:
        x.wait_recv()
    inner = pl.ds(PAD, CR)
    KP[1:S + 1, PAD:PAD + CR, :] = GK[...]
    lane = lax.broadcasted_iota(jnp.int32, (CR, mcols), 1)
    first = lane < half
    z_lo = (lane == 0) | (lane == half)
    z_hi = (lane == half - 1) | (lane == mcols - 1)

    def neighbours(ref, i, roll_i, roll_m, roll_p):
        v0 = ref[i, inner, :]
        return (
            roll_i,
            jnp.where(first, roll_m, roll_p),
            ref[i, pl.ds(PAD - 1, CR), :],
            ref[i, pl.ds(PAD + 1, CR), :],
            pltpu.roll(v0, 1, 1),
            pltpu.roll(v0, mcols - 1, 1),
        )

    def swap(ref, i):
        return pltpu.roll(ref[i, inner, :], half, 1)

    for i in range(1, S + 1):
        k0 = KP[i, inner, :]
        near = list(neighbours(KP, i, swap(KP, i), swap(KP, i - 1), swap(KP, i + 1)))
        near[4] = jnp.where(z_lo, 0.0, near[4])
        near[5] = jnp.where(z_hi, 0.0, near[5])
        total = 2.0 * (6.0 * k0 + (((near[0] + near[1]) + (near[2] + near[3])) + (near[4] + near[5])))
        inv = RELAX / total
        for q in range(6):
            w = 2.0 * (k0 + near[q]) * inv
            if q == 4:
                w = jnp.where(z_lo, 0.0, w)
            if q == 5:
                w = jnp.where(z_hi, 0.0, w)
            wts[q, i - 1] = w
        wts[6, i - 1] = inv

    eb1.wait_recv()
    for i in range(HM - 2, HM + mdepth + 2):
        U1[i] = W1[i] * B1[i]
    sweep(K1, F1, B1, W1, U1, V1, 1.0, range(HM - 1, HM + mdepth + 1))

    def mid_residual(j):
        i = HM + j
        return (B1[i] - D1[i] * V1[i] + coupling(K1, F1, V1, i))[PAD:PAD + mrows]

    b2 = to_low(mid_residual)
    stage[1] = b2
    gb = gather(1, GB)
    for x in gb:
        x.start()
    own_block(GB, b2)

    UE1[HM:HM + mdepth, PAD:PAD + mrows, :] = V1[HM:HM + mdepth, PAD:PAD + mrows, :]
    eb1b = Exchange(B1, HM, 2, HM, mdepth, mrows, send_m, recv_m, 2)
    eu1 = Exchange(UE1, HM, 0, HM, mdepth, mrows, send_m, recv_m, 3)
    eu = Exchange(UE, HF, 0, 3, depth, rows, send_f, recv_f, 2, corners=False)
    euc = Corners(1, (UE,))
    euc.pack()

    for x in gb:
        x.wait_recv()
    eb1b.start()
    eu1.start()
    eu.start()
    euc.start()
    for i in range(S):
        const = wts[6, i] * GB[i]
        wts[6, i] = const
        va[i + 1, inner, :] = const

    def coarse_sweep(src, dst):
        prev, here = swap(src, 0), swap(src, 1)
        for i in range(1, S + 1):
            nxt = swap(src, i + 1)
            near = neighbours(src, i, here, prev, nxt)
            acc = [wts[q, i - 1] * near[q] for q in range(6)]
            dst[i, inner, :] = (
                ((acc[0] + acc[1]) + (acc[2] + acc[3]))
                + ((acc[4] + acc[5]) + (KEEP * src[i, inner, :] + wts[6, i - 1]))
            )
            prev, here = here, nxt

    @pl.loop(0, (ITERS_C - 1) // 2)
    def _(t):
        coarse_sweep(va, vb)
        coarse_sweep(vb, va)

    coarse_sweep(va, vb)

    eb1b.wait_recv()
    eu1.wait_recv()
    grow_low = [
        select_matrix(mcols, mcols, lambda r, q, p=p: (q == 2 * (r - p * half)) | (q == 2 * (r - p * half) + 1))
        for p in range(2)
    ]
    window = crows + 2 * PAD
    rows_low = select_matrix(MY, window, lambda r, q: (r == 2 * (q - PAD // 2)) | (r == 2 * (q - PAD // 2) + 1))
    tall = jnp.concatenate(
        [
            dot(rows_low, vb[s + n, pl.ds(pl.multiple_of(c * crows, crows), window), :])
            for n in range(3)
        ],
        axis=0,
    )
    for p in range(2):
        grown = dot(tall, grow_low[p])
        for n in range(3):
            for e in range(2):
                i = 4 * n + 2 * p + e
                U1[i] = UE1[i] + grown[n * MY:(n + 1) * MY]
    sweep(K1, F1, B1, W1, U1, V1, 1.0, range(HM - 3, HM + mdepth + 3))
    sweep(K1, F1, B1, W1, V1, U1, 1.0, range(HM - 2, HM + mdepth + 2))

    eu.wait_recv()
    euc.receive()
    grow_z = select_matrix(mcols, cols, lambda r, q: (q == 2 * r) | (q == 2 * r + 1))
    rows_mid = select_matrix(FY, MY, lambda r, q: (r == 2 * (q - PAD // 2)) | (r == 2 * (q - PAD // 2) + 1))
    mids = range(HM - 2, HM + mdepth + 2)
    all_grown = dot(jnp.concatenate([dot(rows_mid, U1[m]) for m in mids], axis=0), grow_z)
    for q, m in enumerate(mids):
        grown = all_grown[q * FY:(q + 1) * FY]
        for i in (2 * (m - HM) + HF, 2 * (m - HM) + HF + 1):
            if 0 <= i < depth + 2 * HF:
                V[i] = UE[i] + grown
    sweep(K, FF, B, W, V, U, 0.5, range(HF - 2, HF + depth + 2))
    sweep(K, FF, B, W, U, V, 0.5, range(HF - 1, HF + depth + 1))

    for j in range(depth):
        i = HF + j
        p_out[j] = V[i, own, :]
        r_out[j] = fine_residual(i)[PAD:PAD + rows]

    for e in (ek, eb, ec, ek1, eb1, eb1b, eu1, eu, euc):
        e.wait_send()
    for x in gk + gb:
        x.wait_send()


def hand_over(p_in, r_in, p_out, r_out, sems):
    copies = [
        pltpu.make_async_copy(p_in, p_out, sems.at[0]),
        pltpu.make_async_copy(r_in, r_out, sems.at[1]),
    ]
    for x in copies:
        x.start()
    for x in copies:
        x.wait()


def local(S, C, divergence, inverse_density):
    depth, rows, cols = divergence.shape
    mdepth, mrows, mcols = depth // 2, rows // 2, cols // 2
    crows = mrows // 2
    fine = pltpu.VMEM((depth + 2 * HF, rows + 2 * PAD, cols), F32)
    mid = pltpu.VMEM((mdepth + 2 * HM, mrows + 2 * PAD, mcols), F32)
    low = pltpu.VMEM((S, crows * C, mcols), F32)
    wide = pltpu.VMEM((S + 2, crows * C + 2 * PAD, mcols), F32)
    n = len(DIRS)
    peers = S * C - 1
    dma = pltpu.SemaphoreType.DMA
    out = jax.ShapeDtypeStruct(divergence.shape, F32)
    inner = pl.pallas_call(
        functools.partial(kernel, S, C),
        out_shape=(out, out),
        in_specs=[pl.BlockSpec(memory_space=pl.ANY)] * 2,
        out_specs=(pl.BlockSpec(memory_space=pltpu.VMEM),) * 2,
        scratch_shapes=[fine] * 7 + [mid] * 7 + [
            pltpu.VMEM((2, crows, mcols), F32), low, low, wide, wide, wide,
            pltpu.VMEM((7, S, crows * C, mcols), F32),
            pltpu.VMEM((mdepth * rows, cols), F32),
            pltpu.VMEM((mdepth * rows, mcols), F32),
            pltpu.VMEM((2, 4, 8, cols), F32), pltpu.VMEM((2, 4, 8, cols), F32),
            pltpu.VMEM((4,) + fine.shape, F32), pltpu.VMEM((4,) + mid.shape, F32),
            dma((2,)), dma((3, n)), dma((3, n)), dma((4, n)), dma((4, n)),
            dma((2, peers)), dma((2, peers)), dma((2, 4)), dma((2, 4)),
            pltpu.SemaphoreType.REGULAR((max(S, C).bit_length(),)),
        ],
        compiler_params=pltpu.CompilerParams(collective_id=0, has_side_effects=True),
    )(divergence, inverse_density)
    return pl.pallas_call(
        hand_over,
        out_shape=(out, out),
        in_specs=[pl.BlockSpec(memory_space=pltpu.VMEM)] * 2,
        out_specs=(pl.BlockSpec(memory_space=pl.ANY),) * 2,
        scratch_shapes=[dma((2,))],
    )(*inner)


def solution(mesh):
    placed = P("span", "cross", None)
    return jax.shard_map(
        functools.partial(local, mesh.shape["span"], mesh.shape["cross"]),
        mesh=mesh,
        in_specs=(placed, placed),
        out_specs=(placed, placed),
        check_vma=False,
    )
```

profile of v0, /device:TPU:0, one launch (start us, length us, event | category | flops | bytes accessed | tf_op | source)
XLA Modules:
  0.0 45.5 jit_solution(12944952473531331192)
XLA Ops:
  0.6 43.0 %shard_map.41 = (f32[8,32,256]{2,1,0:T(8,128)}, f32[8,32,256]{2,1,0:T(8,128)}) custom-call(f32[8,32,256]{2,1,0:T(8,128)} %b_hbm.1, f32[8,32,256]{2,1,0:T(8,128)} %k_hbm.1), custom_call_target="tpu_custom_call" | custom-call | tf_op jit(solution)/shard_map/pallas_call | solution.py:526
  43.7 1.8 %shard_map.42 = (f32[8,32,256]{2,1,0:T(8,128)}, f32[8,32,256]{2,1,0:T(8,128)}) custom-call(f32[8,32,256]{2,1,0:T(8,128)} %get-tuple-element.4.p_in, f32[8,32,256]{2,1,0:T(8,128)} %get-tuple-element.5.r_in), custom_call_target="tpu_custom_call" | custom-call | tf_op jit(solution)/shard_map/pallas_call | solution.py:544
where the time goes:
time: 45.7 us; the launch traced here: 45.5 us
  Pallas kernels  44.9 us (98%)
  between operations  0.64 us (1%)
    pallas_call x1, Pallas kernels, local(): pl.pallas_call(functools.partial(kernel, S, C), out_shape=(out, out), in_...  43 us
    pallas_call x1, Pallas kernels, local(): pl.pallas_call(hand_over, out_shape=(out, out), in_specs=[pl.BlockSpec(me...  1.83 us

commit v1 on v0

--- a/solution.py
+++ b/solution.py
@@ -13,6 +13,9 @@
 HF = 3
 HM = 4
 PAD = 8
+Q = 4
+A = Q // 2
+MC = HM - 1
 DIRS = [(dx, dy) for dx in (-1, 0, 1) for dy in (-1, 0, 1) if (dx, dy) != (0, 0)]
 HI = lax.Precision.HIGHEST
 F32 = jnp.float32
@@ -31,15 +34,17 @@
 def kernel(S, C, b_hbm, k_hbm, p_out, r_out,
            K, B, U, V, W, DD, UE, K1, B1, U1, V1, W1, D1, UE1,
            stage, GK, GB, KP, va, vb, wts, t256, t128,
-           corner_out, corner_in, FF, F1,
-           load_sem, send_f, recv_f, send_m, recv_m, send_g, recv_g, send_c, recv_c, known):
+           corner_out, corner_in, mid_out, mid_in, FF, F1,
+           load_sem, send_f, recv_f, send_m, recv_m, send_g, recv_g, send_c, recv_c, send_k, recv_k, known):
     depth, rows, cols = b_hbm.shape
     FY = rows + 2 * PAD
     mdepth, mrows, mcols = depth // 2, rows // 2, cols // 2
     MY = mrows + 2 * PAD
     crows = mrows // 2
     CR = crows * C
-    half = mcols // 2
+    zw = mcols // Q
+    XI = 2 * S // Q
+    NV = XI * A
     s = lax.axis_index("span")
     c = lax.axis_index("cross")
 
@@ -90,10 +95,10 @@
         return sl, dl, ln, sr, dr, rn
 
     class Exchange:
-        def __init__(self, buf, halo, h0, h1, n, r, ssem, rsem, slot, source=None, corners=True):
+        def __init__(self, buf, halo, h0, h1, n, r, ssem, rsem, slot, source=None, corners=True, along=False):
             self.items = []
             for q, (dx, dy) in enumerate(DIRS):
-                if (dx == 0 and h0 > 0) or (dx != 0 and dy != 0 and not corners):
+                if (dx == 0 and h0 > 0 and not along) or (dx != 0 and dy != 0 and not corners):
                     continue
                 sl, dl, ln, sr, dr, rn = spans(dx, dy, halo, h0, h1, n, r)
                 if source is None:
@@ -200,7 +205,69 @@
                 def _(copy=copy):
                     copy.wait_send()
 
+    class MidCorners:
+        def __init__(self, slot, buf):
+            self.slot, self.buf, self.items = slot, buf, []
+            for q, (dx, dy) in enumerate((i, j) for i in (-1, 1) for j in (-1, 1)):
+                copy = pltpu.make_async_remote_copy(
+                    src_ref=mid_out.at[slot, q],
+                    dst_ref=mid_in.at[slot, q],
+                    send_sem=send_k.at[slot, q],
+                    recv_sem=recv_k.at[slot, q],
+                    device_id=(jnp.clip(s + dx, 0, S - 1), jnp.clip(c + dy, 0, C - 1)),
+                    device_id_type=pl.DeviceIdType.MESH,
+                )
+                self.items.append((q, dx, dy, copy))
+
+        def pack(self):
+            for q, dx, dy, copy in self.items:
+                at = 0
+                for e in range(1, MC + 1):
+                    n = MC + 1 - e
+                    layer = HM + mdepth - e if dx == 1 else HM + e - 1
+                    row = PAD + mrows - n if dy == 1 else PAD
+                    mid_out[self.slot, q, at:at + n, :] = self.buf[layer, row:row + n, :]
+                    at += n
+
+        def start(self):
+            for q, dx, dy, copy in self.items:
+                @pl.when(exists(dx, dy))
+                def _(copy=copy):
+                    copy.start()
+
+        def receive(self):
+            for q, dx, dy, copy in self.items:
+                @pl.when(exists(-dx, -dy))
+                def _(q=q, dx=dx, dy=dy, copy=copy):
+                    copy.wait_recv()
+                    at = 0
+                    for e in range(1, MC + 1):
+                        n = MC + 1 - e
+                        layer = HM - e if dx == 1 else HM + mdepth + e - 1
+                        row = PAD - n if dy == 1 else PAD + mrows
+                        self.buf[layer, row:row + n, :] = mid_in[self.slot, q, at:at + n, :]
+                        at += n
+
+        def wait_send(self):
+            for q, dx, dy, copy in self.items:
+                @pl.when(exists(dx, dy))
+                def _(copy=copy):
+                    copy.wait_send()
+
     heard(barrier, 1)
+    steps = []
+    while 2 ** len(steps) < max(S, C) - 1:
+        steps.append(2 ** len(steps))
+    pending = list(enumerate(steps))
+
+    def meet(rounds):
+        for _ in range(min(rounds, len(pending))):
+            turn, step = pending.pop(0)
+            heard(known.at[turn], step)
+            if pending:
+                greet(known.at[pending[0][0]], pending[0][1])
+
+    greet(known.at[0], steps[0])
     ek = Exchange(K, HF, 0, 3, depth, rows, send_f, recv_f, 0, k_hbm, corners=False)
     eb = Exchange(B, HF, 0, 2, depth, rows, send_f, recv_f, 1, b_hbm, corners=False)
     ek.start()
@@ -212,26 +279,27 @@
     ec.pack()
     ec.start()
 
-    step, turn = 1, 0
-    while step < max(S, C) - 1:
-        greet(known.at[turn], step)
-        heard(known.at[turn], step)
-        step, turn = 2 * step, turn + 1
-
     for buf in (K, B, UE):
         for i in (0, HF + depth):
             for j in (0, PAD + rows):
                 buf[i:i + HF, j:j + PAD, :] = jnp.zeros((HF, PAD, cols), F32)
         zero_edges(buf, HF, depth, rows)
-    for buf in (K1, B1, UE1):
+    mid_out[...] = jnp.zeros(mid_out.shape, F32)
+    for buf, value in ((K1, 1.0), (B1, 0.0), (UE1, 0.0)):
+        for i in (0, HM + mdepth):
+            for j in (0, PAD + mrows):
+                buf[i:i + HM, j:j + PAD, :] = jnp.full((HM, PAD, mcols), value, F32)
         zero_edges(buf, HM, mdepth, mrows)
     KP[...] = jnp.zeros(KP.shape, F32)
     va[...] = jnp.zeros(va.shape, F32)
     vb[...] = jnp.zeros(vb.shape, F32)
 
     pair_z = select_matrix(cols, mcols, lambda r, q: (r == 2 * q) | (r == 2 * q + 1))
+    def cell(q):
+        return (q % zw) * A + (q // zw) % A
+
     low = [
-        select_matrix(mcols, mcols, lambda r, q, p=p: (r == 2 * (q - p * half)) | (r == 2 * (q - p * half) + 1))
+        select_matrix(mcols, mcols, lambda r, q, p=p: (r // 2 == cell(q)) & (q // (A * zw) == p))
         for p in range(2)
     ]
 
@@ -251,7 +319,9 @@
         )
     t128[...] = dot(t256[...], pair_z)
     K1[HM:HM + mdepth, PAD:PAD + mrows, :] = (0.125 * restrict_rows(mdepth * mrows)).reshape(mdepth, mrows, mcols)
-    ek1 = Exchange(K1, HM, 0, HM, mdepth, mrows, send_m, recv_m, 0)
+    ek1 = Exchange(K1, HM, 0, HM, mdepth, mrows, send_m, recv_m, 0, corners=False)
+    ek1c = MidCorners(0, K1)
+    ek1c.pack()
 
     def gather(slot, dst):
         row = pl.multiple_of(c * crows, crows)
@@ -331,15 +401,18 @@
     in_d, out_d = split(HF - 2, end + 2, HF + 1, end - 1)
     in_u, out_u = split(HF - 1, end + 1, HF + 2, end - 2)
     in_r, out_r = split(0, mdepth, 2, mdepth - 2)
+    meet(1)
     ek.wait_recv(0)
     eb.wait_recv(0)
     fine_start(in_d)
     sweep(K, FF, B, W, U, V, 0.5, in_u)
     fine_pairs(in_r)
+    meet(len(steps))
     ek.wait_recv(1)
     eb.wait_recv(1)
     ec.receive()
     ek1.start()
+    ek1c.start()
     for x in gk:
         x.start()
     fine_start(out_d)
@@ -348,11 +421,15 @@
 
     t128[...] = dot(t256[...], pair_z)
     B1[HM:HM + mdepth, PAD:PAD + mrows, :] = restrict_rows(mdepth * mrows).reshape(mdepth, mrows, mcols)
-    eb1 = Exchange(B1, HM, 0, 2, mdepth, mrows, send_m, recv_m, 1)
+    eb1 = Exchange(B1, HM, 0, MC, mdepth, mrows, send_m, recv_m, 1, corners=False)
     eb1.start()
-
-    UE[HF:HF + depth, PAD:PAD + rows, :] = V[HF:HF + depth, PAD:PAD + rows, :]
+    eb1c = MidCorners(1, B1)
+    eb1c.pack()
+    eb1c.start()
+
+    UE[HF - 1:HF + depth + 1, PAD:PAD + rows, :] = V[HF - 1:HF + depth + 1, PAD:PAD + rows, :]
     ek1.wait_recv()
+    ek1c.receive()
 
     for i in range(HM - 3, HM + mdepth + 3):
         total, inv = diagonal(K1, F1, i, 1.0, HM, mdepth, mrows)
@@ -362,43 +439,75 @@
     for x in gk:
         x.wait_recv()
     inner = pl.ds(PAD, CR)
-    KP[1:S + 1, PAD:PAD + CR, :] = GK[...]
     lane = lax.broadcasted_iota(jnp.int32, (CR, mcols), 1)
-    first = lane < half
-    z_lo = (lane == 0) | (lane == half)
-    z_hi = (lane == half - 1) | (lane == mcols - 1)
-
-    def neighbours(ref, i, roll_i, roll_m, roll_p):
-        v0 = ref[i, inner, :]
+    block = lane // zw
+    z_lo = lane % zw == 0
+    z_hi = lane % zw == zw - 1
+
+    def arrange(src, x, a):
+        group = (x % 2) * A + a
+        out = None
+        for q in range(Q):
+            v = src[q * (S // Q) + x // 2]
+            if q != group:
+                v = pltpu.roll(v, ((q - group) * zw) % mcols, 1)
+            out = v if out is None else jnp.where(block == q, v, out)
+        return out
+
+    def neighbours(ref, x, a, fields):
+        before, here, after = fields
+        i = x * A + a
         return (
-            roll_i,
-            jnp.where(first, roll_m, roll_p),
+            before[a],
+            after[a],
             ref[i, pl.ds(PAD - 1, CR), :],
             ref[i, pl.ds(PAD + 1, CR), :],
-            pltpu.roll(v0, 1, 1),
-            pltpu.roll(v0, mcols - 1, 1),
+            here[a - 1] if a > 0 else pltpu.roll(here[A - 1], 1, 1),
+            here[a + 1] if a < A - 1 else pltpu.roll(here[0], mcols - 1, 1),
         )
 
-    def swap(ref, i):
-        return pltpu.roll(ref[i, inner, :], half, 1)
-
-    for i in range(1, S + 1):
-        k0 = KP[i, inner, :]
-        near = list(neighbours(KP, i, swap(KP, i), swap(KP, i - 1), swap(KP, i + 1)))
-        near[4] = jnp.where(z_lo, 0.0, near[4])
-        near[5] = jnp.where(z_hi, 0.0, near[5])
-        total = 2.0 * (6.0 * k0 + (((near[0] + near[1]) + (near[2] + near[3])) + (near[4] + near[5])))
-        inv = RELAX / total
-        for q in range(6):
-            w = 2.0 * (k0 + near[q]) * inv
-            if q == 4:
-                w = jnp.where(z_lo, 0.0, w)
-            if q == 5:
-                w = jnp.where(z_hi, 0.0, w)
-            wts[q, i - 1] = w
-        wts[6, i - 1] = inv
+    def layer(ref, x):
+        return [ref[x * A + a, inner, :] for a in range(A)]
+
+    def columns(ref):
+        first, last = layer(ref, 0), layer(ref, XI - 1)
+        before = [pltpu.roll(v, zw, 1) for v in last]
+        wrap = [pltpu.roll(v, mcols - zw, 1) for v in first]
+        here = first
+        for x in range(XI):
+            after = (last if x + 1 == XI - 1 else layer(ref, x + 1)) if x < XI - 1 else wrap
+            yield x, (before, here, after)
+            before, here = here, after
+
+    for x in range(XI):
+        for a in range(A):
+            KP[x * A + a, inner, :] = arrange(GK, x, a)
+    for x, fields in columns(KP):
+        for a in range(A):
+            k0 = fields[1][a]
+            near = list(neighbours(KP, x, a, fields))
+            outside = {}
+            if x == 0:
+                outside[0] = block == 0
+            if x == XI - 1:
+                outside[1] = block == Q - 1
+            if a == 0:
+                outside[4] = z_lo
+            if a == A - 1:
+                outside[5] = z_hi
+            for q, mask in outside.items():
+                near[q] = jnp.where(mask, 0.0, near[q])
+            total = 2.0 * (6.0 * k0 + (((near[0] + near[1]) + (near[2] + near[3])) + (near[4] + near[5])))
+            inv = RELAX / total
+            for q in range(6):
+                w = 2.0 * (k0 + near[q]) * inv
+                if q in outside:
+                    w = jnp.where(outside[q], 0.0, w)
+                wts[q, x * A + a] = w
+            wts[6, x * A + a] = inv
 
     eb1.wait_recv()
+    eb1c.receive()
     for i in range(HM - 2, HM + mdepth + 2):
         U1[i] = W1[i] * B1[i]
     sweep(K1, F1, B1, W1, U1, V1, 1.0, range(HM - 1, HM + mdepth + 1))
@@ -414,35 +523,37 @@
         x.start()
     own_block(GB, b2)
 
-    UE1[HM:HM + mdepth, PAD:PAD + mrows, :] = V1[HM:HM + mdepth, PAD:PAD + mrows, :]
-    eb1b = Exchange(B1, HM, 2, HM, mdepth, mrows, send_m, recv_m, 2)
-    eu1 = Exchange(UE1, HM, 0, HM, mdepth, mrows, send_m, recv_m, 3)
-    eu = Exchange(UE, HF, 0, 3, depth, rows, send_f, recv_f, 2, corners=False)
+    UE1[HM - 1:HM + mdepth + 1, PAD:PAD + mrows, :] = V1[HM - 1:HM + mdepth + 1, PAD:PAD + mrows, :]
+    eu1 = Exchange(UE1, HM, 1, HM, mdepth, mrows, send_m, recv_m, 2, corners=False, along=True)
+    eu1c = MidCorners(2, UE1)
+    eu1c.pack()
+    eu = Exchange(UE, HF, 1, HF, depth, rows, send_f, recv_f, 2, corners=False, along=True)
     euc = Corners(1, (UE,))
     euc.pack()
 
     for x in gb:
         x.wait_recv()
-    eb1b.start()
     eu1.start()
+    eu1c.start()
     eu.start()
     euc.start()
-    for i in range(S):
-        const = wts[6, i] * GB[i]
-        wts[6, i] = const
-        va[i + 1, inner, :] = const
+    for x in range(XI):
+        for a in range(A):
+            i = x * A + a
+            const = wts[6, i] * arrange(GB, x, a)
+            wts[6, i] = const
+            va[i, inner, :] = const
 
     def coarse_sweep(src, dst):
-        prev, here = swap(src, 0), swap(src, 1)
-        for i in range(1, S + 1):
-            nxt = swap(src, i + 1)
-            near = neighbours(src, i, here, prev, nxt)
-            acc = [wts[q, i - 1] * near[q] for q in range(6)]
-            dst[i, inner, :] = (
-                ((acc[0] + acc[1]) + (acc[2] + acc[3]))
-                + ((acc[4] + acc[5]) + (KEEP * src[i, inner, :] + wts[6, i - 1]))
-            )
-            prev, here = here, nxt
+        for x, fields in columns(src):
+            for a in range(A):
+                i = x * A + a
+                near = neighbours(src, x, a, fields)
+                acc = [wts[q, i] * near[q] for q in range(6)]
+                dst[i, inner, :] = (
+                    ((acc[0] + acc[1]) + (acc[2] + acc[3]))
+                    + ((acc[4] + acc[5]) + (KEEP * fields[1][a] + wts[6, i]))
+                )
 
     @pl.loop(0, (ITERS_C - 1) // 2)
     def _(t):
@@ -451,21 +562,31 @@
 
     coarse_sweep(va, vb)
 
-    eb1b.wait_recv()
     eu1.wait_recv()
+    eu1c.receive()
     grow_low = [
-        select_matrix(mcols, mcols, lambda r, q, p=p: (q == 2 * (r - p * half)) | (q == 2 * (r - p * half) + 1))
+        select_matrix(mcols, mcols, lambda r, q, p=p: (q // 2 == cell(r)) & (r // (A * zw) == p))
         for p in range(2)
     ]
     window = crows + 2 * PAD
     rows_low = select_matrix(MY, window, lambda r, q: (r == 2 * (q - PAD // 2)) | (r == 2 * (q - PAD // 2) + 1))
-    tall = jnp.concatenate(
-        [
-            dot(rows_low, vb[s + n, pl.ds(pl.multiple_of(c * crows, crows), window), :])
-            for n in range(3)
-        ],
-        axis=0,
-    )
+    wide_block = lax.broadcasted_iota(jnp.int32, (window, mcols), 1) // zw
+
+    def own_pair(n):
+        t = s + n - 1
+        at = lax.rem(t + S, S)
+        q = at // (S // Q)
+        x = 2 * lax.rem(at, S // Q)
+        out = jnp.zeros((window, mcols), F32)
+        for e in range(2):
+            for a in range(A):
+                group = e * A + a
+                v = vb[(x + e) * A + a, pl.ds(pl.multiple_of(c * crows, crows), window), :]
+                v = pltpu.roll(v, lax.rem(group - q + Q, Q) * zw, 1)
+                out = jnp.where((wide_block == group) & (t >= 0) & (t < S), v, out)
+        return out
+
+    tall = jnp.concatenate([dot(rows_low, own_pair(n)) for n in range(3)], axis=0)
     for p in range(2):
         grown = dot(tall, grow_low[p])
         for n in range(3):
@@ -494,7 +615,7 @@
         p_out[j] = V[i, own, :]
         r_out[j] = fine_residual(i)[PAD:PAD + rows]
 
-    for e in (ek, eb, ec, ek1, eb1, eb1b, eu1, eu, euc):
+    for e in (ek, eb, ec, ek1, ek1c, eb1, eb1c, eu1, eu1c, eu, euc):
         e.wait_send()
     for x in gk + gb:
         x.wait_send()
@@ -518,7 +639,7 @@
     fine = pltpu.VMEM((depth + 2 * HF, rows + 2 * PAD, cols), F32)
     mid = pltpu.VMEM((mdepth + 2 * HM, mrows + 2 * PAD, mcols), F32)
     low = pltpu.VMEM((S, crows * C, mcols), F32)
-    wide = pltpu.VMEM((S + 2, crows * C + 2 * PAD, mcols), F32)
+    wide = pltpu.VMEM((S, crows * C + 2 * PAD, mcols), F32)
     n = len(DIRS)
     peers = S * C - 1
     dma = pltpu.SemaphoreType.DMA
@@ -534,9 +655,10 @@
             pltpu.VMEM((mdepth * rows, cols), F32),
             pltpu.VMEM((mdepth * rows, mcols), F32),
             pltpu.VMEM((2, 4, 8, cols), F32), pltpu.VMEM((2, 4, 8, cols), F32),
+            pltpu.VMEM((3, 4, 8, mcols), F32), pltpu.VMEM((3, 4, 8, mcols), F32),
             pltpu.VMEM((4,) + fine.shape, F32), pltpu.VMEM((4,) + mid.shape, F32),
-            dma((2,)), dma((3, n)), dma((3, n)), dma((4, n)), dma((4, n)),
-            dma((2, peers)), dma((2, peers)), dma((2, 4)), dma((2, 4)),
+            dma((2,)), dma((3, n)), dma((3, n)), dma((3, n)), dma((3, n)),
+            dma((2, peers)), dma((2, peers)), dma((2, 4)), dma((2, 4)), dma((3, 4)), dma((3, 4)),
             pltpu.SemaphoreType.REGULAR((max(S, C).bit_length(),)),
         ],
         compiler_params=pltpu.CompilerParams(collective_id=0, has_side_effects=True),

time: 45.7 us -> 43.9 us (0.961)
  Pallas kernels: 44.9 us -> 43.1 us
    pallas_call x1, Pallas kernels: 43 us -> 41.3 us  [local(): pl.pallas_call(functools.partial(kernel, S, C), out_shape=(out, out), in_...]
where the time goes in v1:
time: 43.9 us; the launch traced here: 43.8 us
  Pallas kernels  43.1 us (98%)
  between operations  0.64 us (1%)
    pallas_call x1, Pallas kernels, local(): pl.pallas_call(functools.partial(kernel, S, C), out_shape=(out, out), in_...  41.3 us
    pallas_call x1, Pallas kernels, local(): pl.pallas_call(hand_over, out_shape=(out, out), in_specs=[pl.BlockSpec(me...  1.83 us

profile of v1, /device:TPU:0, one launch (start us, length us, event | category | flops | bytes accessed | tf_op | source)
XLA Modules:
  0.0 43.8 jit_solution(10620534919623056294)
XLA Ops:
  0.6 41.3 %shard_map.41 = (f32[8,32,256]{2,1,0:T(8,128)}, f32[8,32,256]{2,1,0:T(8,128)}) custom-call(f32[8,32,256]{2,1,0:T(8,128)} %b_hbm.1, f32[8,32,256]{2,1,0:T(8,128)} %k_hbm.1), custom_call_target="tpu_custom_call" | custom-call | tf_op jit(solution)/shard_map/pallas_call | solution.py:647
  42.0 1.8 %shard_map.42 = (f32[8,32,256]{2,1,0:T(8,128)}, f32[8,32,256]{2,1,0:T(8,128)}) custom-call(f32[8,32,256]{2,1,0:T(8,128)} %get-tuple-element.4.p_in, f32[8,32,256]{2,1,0:T(8,128)} %get-tuple-element.5.r_in), custom_call_target="tpu_custom_call" | custom-call | tf_op jit(solution)/shard_map/pallas_call | solution.py:666

commit v2 on v1

--- a/solution.py
+++ b/solution.py
@@ -254,31 +254,7 @@
                 def _(copy=copy):
                     copy.wait_send()
 
-    heard(barrier, 1)
-    steps = []
-    while 2 ** len(steps) < max(S, C) - 1:
-        steps.append(2 ** len(steps))
-    pending = list(enumerate(steps))
-
-    def meet(rounds):
-        for _ in range(min(rounds, len(pending))):
-            turn, step = pending.pop(0)
-            heard(known.at[turn], step)
-            if pending:
-                greet(known.at[pending[0][0]], pending[0][1])
-
-    greet(known.at[0], steps[0])
-    ek = Exchange(K, HF, 0, 3, depth, rows, send_f, recv_f, 0, k_hbm, corners=False)
-    eb = Exchange(B, HF, 0, 2, depth, rows, send_f, recv_f, 1, b_hbm, corners=False)
-    ek.start()
-    eb.start()
     corner_out[...] = jnp.zeros(corner_out.shape, F32)
-    for x in loads:
-        x.wait()
-    ec = Corners(0, (K, B))
-    ec.pack()
-    ec.start()
-
     for buf in (K, B, UE):
         for i in (0, HF + depth):
             for j in (0, PAD + rows):
@@ -293,6 +269,30 @@
     KP[...] = jnp.zeros(KP.shape, F32)
     va[...] = jnp.zeros(va.shape, F32)
     vb[...] = jnp.zeros(vb.shape, F32)
+
+    heard(barrier, 1)
+    steps = []
+    while 2 ** len(steps) < max(S, C) - 1:
+        steps.append(2 ** len(steps))
+    pending = list(enumerate(steps))
+
+    def meet(rounds):
+        for _ in range(min(rounds, len(pending))):
+            turn, step = pending.pop(0)
+            heard(known.at[turn], step)
+            if pending:
+                greet(known.at[pending[0][0]], pending[0][1])
+
+    greet(known.at[0], steps[0])
+    ek = Exchange(K, HF, 0, 3, depth, rows, send_f, recv_f, 0, k_hbm, corners=False)
+    eb = Exchange(B, HF, 0, 2, depth, rows, send_f, recv_f, 1, b_hbm, corners=False)
+    ek.start()
+    eb.start()
+    for x in loads:
+        x.wait()
+    ec = Corners(0, (K, B))
+    ec.pack()
+    ec.start()
 
     pair_z = select_matrix(cols, mcols, lambda r, q: (r == 2 * q) | (r == 2 * q + 1))
     def cell(q):
@@ -407,14 +407,12 @@
     fine_start(in_d)
     sweep(K, FF, B, W, U, V, 0.5, in_u)
     fine_pairs(in_r)
-    meet(len(steps))
     ek.wait_recv(1)
     eb.wait_recv(1)
     ec.receive()
     ek1.start()
     ek1c.start()
-    for x in gk:
-        x.start()
+    meet(1)
     fine_start(out_d)
     sweep(K, FF, B, W, U, V, 0.5, out_u)
     fine_pairs(out_r)
@@ -426,6 +424,9 @@
     eb1c = MidCorners(1, B1)
     eb1c.pack()
     eb1c.start()
+    meet(len(steps))
+    for x in gk:
+        x.start()
 
     UE[HF - 1:HF + depth + 1, PAD:PAD + rows, :] = V[HF - 1:HF + depth + 1, PAD:PAD + rows, :]
     ek1.wait_recv()
@@ -435,6 +436,31 @@
         total, inv = diagonal(K1, F1, i, 1.0, HM, mdepth, mrows)
         D1[i] = total
         W1[i] = inv
+
+    eb1.wait_recv()
+    eb1c.receive()
+    for i in range(HM - 2, HM + mdepth + 2):
+        U1[i] = W1[i] * B1[i]
+    sweep(K1, F1, B1, W1, U1, V1, 1.0, range(HM - 1, HM + mdepth + 1))
+
+    def mid_residual(j):
+        i = HM + j
+        return (B1[i] - D1[i] * V1[i] + coupling(K1, F1, V1, i))[PAD:PAD + mrows]
+
+    b2 = to_low(mid_residual)
+    stage[1] = b2
+    gb = gather(1, GB)
+    for x in gb:
+        x.start()
+    own_block(GB, b2)
+
+    UE1[HM - 1:HM + mdepth + 1, PAD:PAD + mrows, :] = V1[HM - 1:HM + mdepth + 1, PAD:PAD + mrows, :]
+    eu1 = Exchange(UE1, HM, 1, HM, mdepth, mrows, send_m, recv_m, 2, corners=False, along=True)
+    eu1c = MidCorners(2, UE1)
+    eu1c.pack()
+    eu = Exchange(UE, HF, 1, HF, depth, rows, send_f, recv_f, 2, corners=False, along=True)
+    euc = Corners(1, (UE,))
+    euc.pack()
 
     for x in gk:
         x.wait_recv()
@@ -505,31 +531,6 @@
                     w = jnp.where(outside[q], 0.0, w)
                 wts[q, x * A + a] = w
             wts[6, x * A + a] = inv
-
-    eb1.wait_recv()
-    eb1c.receive()
-    for i in range(HM - 2, HM + mdepth + 2):
-        U1[i] = W1[i] * B1[i]
-    sweep(K1, F1, B1, W1, U1, V1, 1.0, range(HM - 1, HM + mdepth + 1))
-
-    def mid_residual(j):
-        i = HM + j
-        return (B1[i] - D1[i] * V1[i] + coupling(K1, F1, V1, i))[PAD:PAD + mrows]
-
-    b2 = to_low(mid_residual)
-    stage[1] = b2
-    gb = gather(1, GB)
-    for x in gb:
-        x.start()
-    own_block(GB, b2)
-
-    UE1[HM - 1:HM + mdepth + 1, PAD:PAD + mrows, :] = V1[HM - 1:HM + mdepth + 1, PAD:PAD + mrows, :]
-    eu1 = Exchange(UE1, HM, 1, HM, mdepth, mrows, send_m, recv_m, 2, corners=False, along=True)
-    eu1c = MidCorners(2, UE1)
-    eu1c.pack()
-    eu = Exchange(UE, HF, 1, HF, depth, rows, send_f, recv_f, 2, corners=False, along=True)
-    euc = Corners(1, (UE,))
-    euc.pack()
 
     for x in gb:
         x.wait_recv()

time: 43.9 us -> 43.7 us (level)
  no operation moved by 1% of the time
where the time goes in v2:
time: 43.7 us; the launch traced here: 43.5 us
  Pallas kernels  42.9 us (98%)
  between operations  0.64 us (1%)
    pallas_call x1, Pallas kernels, local(): pl.pallas_call(functools.partial(kernel, S, C), out_shape=(out, out), in_...  41 us
    pallas_call x1, Pallas kernels, local(): pl.pallas_call(hand_over, out_shape=(out, out), in_specs=[pl.BlockSpec(me...  1.83 us

profile of v2, /device:TPU:0, one launch (start us, length us, event | category | flops | bytes accessed | tf_op | source)
XLA Modules:
  0.0 43.5 jit_solution(6996581676959371228)
XLA Ops:
  0.6 41.0 %shard_map.41 = (f32[8,32,256]{2,1,0:T(8,128)}, f32[8,32,256]{2,1,0:T(8,128)}) custom-call(f32[8,32,256]{2,1,0:T(8,128)} %b_hbm.1, f32[8,32,256]{2,1,0:T(8,128)} %k_hbm.1), custom_call_target="tpu_custom_call" | custom-call | tf_op jit(solution)/shard_map/pallas_call | solution.py:648
  41.7 1.8 %shard_map.42 = (f32[8,32,256]{2,1,0:T(8,128)}, f32[8,32,256]{2,1,0:T(8,128)}) custom-call(f32[8,32,256]{2,1,0:T(8,128)} %get-tuple-element.4.p_in, f32[8,32,256]{2,1,0:T(8,128)} %get-tuple-element.5.r_in), custom_call_target="tpu_custom_call" | custom-call | tf_op jit(solution)/shard_map/pallas_call | solution.py:667

commit v3 on v2

--- a/solution.py
+++ b/solution.py
@@ -54,8 +54,6 @@
     ]
     for x in loads:
         x.start()
-
-    peers = [(i, j) for i in range(S) for j in range(C) if (i, j) != (0, 0)]
 
     def peer(o):
         return (lax.rem(s + o[0], S), lax.rem(c + o[1], C))
@@ -322,27 +320,63 @@
     ek1 = Exchange(K1, HM, 0, HM, mdepth, mrows, send_m, recv_m, 0, corners=False)
     ek1c = MidCorners(0, K1)
     ek1c.pack()
-
-    def gather(slot, dst):
-        row = pl.multiple_of(c * crows, crows)
-        return [
-            pltpu.make_async_remote_copy(
-                src_ref=stage.at[slot],
-                dst_ref=dst.at[s, pl.ds(row, crows), :],
-                send_sem=send_g.at[slot, n],
-                recv_sem=recv_g.at[slot, n],
-                device_id=peer(o),
-                device_id_type=pl.DeviceIdType.MESH,
-            )
-            for n, o in reversed(list(enumerate(peers)))
-        ]
+    ek1.start()
+    ek1c.start()
+
+    order = sorted(range(1, S), key=lambda i: (min(i, S - i), i))
+
+    class Gather:
+        def __init__(self, slot, dst):
+            rows_c = pl.ds(pl.multiple_of(c * crows, crows), crows)
+
+            def copy(src, at, n, where):
+                return pltpu.make_async_remote_copy(
+                    src_ref=src,
+                    dst_ref=dst.at[at, rows_c, :],
+                    send_sem=send_g.at[slot, n],
+                    recv_sem=recv_g.at[slot, n],
+                    device_id=where,
+                    device_id_type=pl.DeviceIdType.MESH,
+                )
+
+            def onward(src, at, i):
+                return [copy(src, at, S * j + i, peer((0, j))) for j in range(1, C)]
+
+            own = stage.at[slot]
+            self.far = {i: copy(own, s, i, peer((i, 0))) for i in order}
+            self.near = {0: onward(own, s, 0)}
+            for i in order:
+                t = lax.rem(s - i + S, S)
+                self.near[i] = onward(dst.at[t, rows_c, :], t, i)
+
+        def start(self):
+            for i in reversed(order):
+                self.far[i].start()
+            for x in self.near[0]:
+                x.start()
+
+        def wait_recv(self):
+            for i in order:
+                self.far[i].wait_recv()
+                for x in self.near[i]:
+                    x.start()
+            for i in [0] + order:
+                for x in self.near[i]:
+                    x.wait_recv()
+
+        def wait_send(self):
+            for i in order:
+                self.far[i].wait_send()
+            for i in [0] + order:
+                for x in self.near[i]:
+                    x.wait_send()
 
     def own_block(dst, value):
         dst[s, pl.ds(pl.multiple_of(c * crows, crows), crows), :] = value
 
     k2 = 0.125 * to_low(lambda j: K1[HM + j, pl.ds(PAD, mrows), :])
     stage[0] = k2
-    gk = gather(0, GK)
+    gk = Gather(0, GK)
     own_block(GK, k2)
 
     def coupling(Kr, Fr, Vr, i):
@@ -410,8 +444,6 @@
     ek.wait_recv(1)
     eb.wait_recv(1)
     ec.receive()
-    ek1.start()
-    ek1c.start()
     meet(1)
     fine_start(out_d)
     sweep(K, FF, B, W, U, V, 0.5, out_u)
@@ -425,8 +457,7 @@
     eb1c.pack()
     eb1c.start()
     meet(len(steps))
-    for x in gk:
-        x.start()
+    gk.start()
 
     UE[HF - 1:HF + depth + 1, PAD:PAD + rows, :] = V[HF - 1:HF + depth + 1, PAD:PAD + rows, :]
     ek1.wait_recv()
@@ -449,9 +480,8 @@
 
     b2 = to_low(mid_residual)
     stage[1] = b2
-    gb = gather(1, GB)
-    for x in gb:
-        x.start()
+    gb = Gather(1, GB)
+    gb.start()
     own_block(GB, b2)
 
     UE1[HM - 1:HM + mdepth + 1, PAD:PAD + mrows, :] = V1[HM - 1:HM + mdepth + 1, PAD:PAD + mrows, :]
@@ -462,8 +492,7 @@
     euc = Corners(1, (UE,))
     euc.pack()
 
-    for x in gk:
-        x.wait_recv()
+    gk.wait_recv()
     inner = pl.ds(PAD, CR)
     lane = lax.broadcasted_iota(jnp.int32, (CR, mcols), 1)
     block = lane // zw
@@ -532,8 +561,7 @@
                 wts[q, x * A + a] = w
             wts[6, x * A + a] = inv
 
-    for x in gb:
-        x.wait_recv()
+    gb.wait_recv()
     eu1.start()
     eu1c.start()
     eu.start()
@@ -618,8 +646,8 @@
 
     for e in (ek, eb, ec, ek1, ek1c, eb1, eb1c, eu1, eu1c, eu, euc):
         e.wait_send()
-    for x in gk + gb:
-        x.wait_send()
+    gk.wait_send()
+    gb.wait_send()
 
 
 def hand_over(p_in, r_in, p_out, r_out, sems):
@@ -642,7 +670,7 @@
     low = pltpu.VMEM((S, crows * C, mcols), F32)
     wide = pltpu.VMEM((S, crows * C + 2 * PAD, mcols), F32)
     n = len(DIRS)
-    peers = S * C - 1
+    peers = S * C
     dma = pltpu.SemaphoreType.DMA
     out = jax.ShapeDtypeStruct(divergence.shape, F32)
     inner = pl.pallas_call(

time: 43.7 us -> 44.3 us (1.014)
  Pallas kernels: 42.9 us -> 43.5 us
    pallas_call x1, Pallas kernels: 41 us -> 41.7 us  [local(): pl.pallas_call(functools.partial(kernel, S, C), out_shape=(out, out), in_...]
where the time goes in v3:
time: 44.3 us; the launch traced here: 44.1 us
  Pallas kernels  43.5 us (98%)
  between operations  0.64 us (1%)
    pallas_call x1, Pallas kernels, local(): pl.pallas_call(functools.partial(kernel, S, C), out_shape=(out, out), in_...  41.7 us
    pallas_call x1, Pallas kernels, local(): pl.pallas_call(hand_over, out_shape=(out, out), in_specs=[pl.BlockSpec(me...  1.83 us

profile of v3, /device:TPU:0, one launch (start us, length us, event | category | flops | bytes accessed | tf_op | source)
XLA Modules:
  0.0 44.1 jit_solution(7161848183476777145)
XLA Ops:
  0.6 41.7 %shard_map.41 = (f32[8,32,256]{2,1,0:T(8,128)}, f32[8,32,256]{2,1,0:T(8,128)}) custom-call(f32[8,32,256]{2,1,0:T(8,128)} %b_hbm.1, f32[8,32,256]{2,1,0:T(8,128)} %k_hbm.1), custom_call_target="tpu_custom_call" | custom-call | tf_op jit(solution)/shard_map/pallas_call | solution.py:676
  42.3 1.8 %shard_map.42 = (f32[8,32,256]{2,1,0:T(8,128)}, f32[8,32,256]{2,1,0:T(8,128)}) custom-call(f32[8,32,256]{2,1,0:T(8,128)} %get-tuple-element.4.p_in, f32[8,32,256]{2,1,0:T(8,128)} %get-tuple-element.5.r_in), custom_call_target="tpu_custom_call" | custom-call | tf_op jit(solution)/shard_map/pallas_call | solution.py:695
